TPU v7x, 32 devices: a whole 2x2x4 slice. The times are simulated.
32 devices in a mesh: lsec: 4 (over y, x), rsec: 8 (over z, core).
Axes of the slice: x: 2, y: 2, z: 4, core: 2. Of those that a mesh axis runs over, the one named last changes fastest.
Arguments:
- psi: bfloat16 [16, 16, 256, 256], P('lsec', 'rsec'), may hold values from -6 to 6
- left_env: bfloat16 [16, 4, 256, 256], P('lsec'), may hold values from -0.375 to 0.375
- right_env: bfloat16 [16, 4, 256, 256], P('rsec'), may hold values from -0.1875 to 0.1875
- energies: float32 [16, 16], P('lsec', 'rsec'), may hold values from 0.5 to 3
- coef_num: int32 [2], replicated, may hold values from 3 to 9
- coef_den: int32 [2], replicated, may hold values from 4 to 8
Outputs:
- vector_out: bfloat16 [16, 16, 256, 256], P('lsec', 'rsec')
- ritz: float32 [3], replicated
All inputs are finite; a program needn't handle non-finite values.
Results may differ from a plain program's by a relative error of at most 0.015.
Values may be sent and summed in bfloat16 or wider, within the bound.
A program may use at most 64 MiB of HBM per device.

v0:
```python
import jax
import jax.numpy as jnp
from jax import lax
from jax.sharding import PartitionSpec as P

DIAG = 2
HOPS = 1
ITERS = 3


eps = 1e-06


def padded(block, sides, width):
    for axis, dim in sides:
        count = lax.axis_size(axis)
        forward = [(i, i + 1) for i in range(count - 1)]
        backward = [(target, source) for source, target in forward]
        low = lax.ppermute(
            lax.slice_in_dim(block, block.shape[dim] - width, None, axis=dim), axis, forward
        )
        high = lax.ppermute(lax.slice_in_dim(block, 0, width, axis=dim), axis, backward)
        block = jnp.concatenate([low, block, high], axis=dim)
    return block


def add_terms(left_env, right_env, source, first, number, total):
    for term in range(first, first + number):
        inner = jnp.einsum(
            "aij,abjk->abik", left_env[:, term], source, preferred_element_type=jnp.float32
        ).astype(jnp.bfloat16)
        total = total + jnp.einsum(
            "abik,blk->abil", inner, right_env[:, term], preferred_element_type=jnp.float32
        )
    return total


def with_rims(vec):
    wide = padded(vec, (("rsec", 1),), 1)
    full = padded(wide, (("lsec", 0),), 1)
    return full


def matvec(vec, left_env, right_env, energies):
    vals = vec.astype(jnp.float32)
    total = energies[:, :, None, None] * vals
    total = add_terms(left_env, right_env, vec, 0, DIAG, total)
    full = with_rims(vec)
    plus_blocks = full[:-2, 2:]
    minus_blocks = full[2:, :-2]
    total = add_terms(left_env, right_env, plus_blocks, DIAG, HOPS, total)
    total = add_terms(left_env, right_env, minus_blocks, DIAG + HOPS, HOPS, total)
    return total


def per_device(psi, left_env, right_env, energies, coef_num, coef_den):
    count = 1.0 / float(psi.size * lax.axis_size("lsec") * lax.axis_size("rsec"))
    start_vals = psi.astype(jnp.float32)
    start = lax.psum(jnp.sum(start_vals * start_vals), ("lsec", "rsec")) * count
    vec = (start_vals * lax.rsqrt(start + eps)).astype(jnp.bfloat16)
    previous = jnp.zeros(psi.shape, jnp.float32)
    thetas = []
    for step in range(ITERS):
        sigma = matvec(vec, left_env, right_env, energies)
        vals = vec.astype(jnp.float32)
        if step == 0:
            coef = jnp.float32(0.0)
        else:
            coef = coef_num[step - 1].astype(jnp.float32) / coef_den[step - 1].astype(jnp.float32)
        sums = lax.psum(
            (
                jnp.sum(sigma * sigma),
                jnp.sum(sigma * vals),
                jnp.sum(sigma * previous),
                jnp.sum(vals * vals),
                jnp.sum(vals * previous),
                jnp.sum(previous * previous),
            ),
            ("lsec", "rsec"),
        )
        m_ss, m_sv, m_sp, m_vv, m_vp, m_pp = [part * count for part in sums]
        resid = sigma - m_sv * vals - coef * previous
        norm_sq = (
            m_ss
            - 2.0 * m_sv * m_sv
            - 2.0 * coef * m_sp
            + m_sv * m_sv * m_vv
            + 2.0 * m_sv * coef * m_vp
            + coef * coef * m_pp
        )
        thetas.append(m_sv)
        previous = vals
        vec = (resid * lax.rsqrt(norm_sq + eps)).astype(jnp.bfloat16)
    return (vec, jnp.stack(thetas))


def solution(mesh):
    in_specs = (
        P("lsec", "rsec", None, None),
        P("lsec", None, None, None),
        P("rsec", None, None, None),
        P("lsec", "rsec"),
        P(),
        P(),
    )
    out_specs = (P("lsec", "rsec", None, None), P())
    return jax.shard_map(
        per_device, mesh=mesh, in_specs=in_specs, out_specs=out_specs, check_vma=False
    )
```

profile of v0, /device:TPU:0, one launch (start us, length us, event | category | flops | bytes accessed | tf_op | source)
XLA Modules:
  0.0 343.5 jit_solution(12554492794385849762)
XLA Ops:
  0.6 2.4 fusion
  3.0 42.2 %psum.125 = f32[]{:T(128)} all-reduce(f32[]{:T(128)} %fusion), channel_id=1, replica_groups=mesh['lsec'=4,'rsec'=8] {'lsec','rsec'}, use_global_device_ids=true, to_apply=%region_1.0 | all-reduce | flops 1 | bytes 8 | tf_op jit(solution)/shard_map/psum | solution.py:59
  47.4 1.5 collective-permute-start
  50.3 4.0 %collective-permute-done.1 = bf16[4,1,256,256]{3,2,0,1:T(8,128)(2,1)S(1)} collective-permute-done((bf16[4,1,256,256]{3,2,0,1:T(8,128)(2,1)S(1)}, bf16[4,1,256,256]{3,2,0,1:T(8,128)(2,1)S(1)}, u32[]{:S(2)}, u32[]{:S(2)}) %collective-permute-start.1) | collective-permute-done | bytes 524320 | tf_op jit(solution)/shard_map/ppermute | solution.py:22
  55.5 5.0 %collective-permute-start.2 = (bf16[1,4,256,256]{3,2,0,1:T(8,128)(2,1)}, bf16[1,4,256,256]{3,2,0,1:T(8,128)(2,1)}, u32[]{:S(2)}, u32[]{:S(2)}) collective-permute-start(bf16[1,4,256,256]{3,2,0,1:T(8,128)(2,1)} %get-tuple-element.40), channel_id=1, source_target_pairs={{0,8},{8,16},{16,24},{1,9},{9,17},{17,25},{2,10},{10,18},{18,26},{... | collective-permute-start | bytes 1572872 | tf_op jit(solution)/shard_map/ppermute | solution.py:19
  60.5 3.0 fusion.37
  64.7 3.0 fusion.39
  67.8 3.2 fusion.41
  71.0 9.3 %collective-permute-done.3 = bf16[1,4,256,256]{3,2,0,1:T(8,128)(2,1)} collective-permute-done((bf16[1,4,256,256]{3,2,0,1:T(8,128)(2,1)}, bf16[1,4,256,256]{3,2,0,1:T(8,128)(2,1)}, u32[]{:S(2)}, u32[]{:S(2)}) %collective-permute-start.3) | collective-permute-done | bytes 524320 | tf_op jit(solution)/shard_map/ppermute | solution.py:22
  80.3 6.9 %multiply_reduce_fusion.2 = (f32[]{:T(128)}, f32[]{:T(128)}, f32[]{:T(128)}, f32[]{:T(128)}, f32[]{:T(128)}, /*index=5*/f32[4,2,256,256]{3,2,0,1:T(8,128)}) fusion(bf16[4,2,256,256]{3,2,0,1:T(8,128)(2,1)S(1)} %fusion.1, bf16[2,4,256,256]{3,2,1,0:T(8,128)(2,1)} %param.8, bf16[1,4,256,256]{3,2,0,1:T(8,128)(2,1)} %collective-permute-done.3, ...), kind=kOutput, calls=%fused_computation.59 | convolution fusion | flops 549978112 | bytes 12846100 | tf_op jit(solution)/shard_map/abik,blk->abil/dot_general | solution.py:32
  87.2 50.7 %all-reduce.2 = (f32[]{:T(128)}, f32[]{:T(128)}, f32[]{:T(128)}, f32[]{:T(128)}, f32[]{:T(128)}, /*index=5*/f32[]{:T(128)}) all-reduce(f32[]{:T(128)} %get-tuple-element.13, f32[]{:T(128)} %get-tuple-element.14, f32[]{:T(128)} %get-tuple-element.12, f32[]{:T(128)} %get-tuple-element.16, ...), channel_id=1, replica_groups=mesh['lsec'=4,'rsec'=8] {'lsec','rsec'}, use_global_device_ids=true, to_apply=%region_5.0 | all-reduce | flops 6 | bytes 48 | tf_op jit(solution)/shard_map/psum | solution.py:70
  143.8 2.0 fusion.19
  146.9 2.1 collective-permute-start.4
  153.5 2.2 pad_maximum_fusion.57
  155.6 5.0 %collective-permute-start.6 = (bf16[1,4,256,256]{3,2,0,1:T(8,128)(2,1)}, bf16[1,4,256,256]{3,2,0,1:T(8,128)(2,1)}, u32[]{:S(2)}, u32[]{:S(2)}) collective-permute-start(bf16[1,4,256,256]{3,2,0,1:T(8,128)(2,1)} %get-tuple-element.38), channel_id=1, source_target_pairs={{0,8},{8,16},{16,24},{1,9},{9,17},{17,25},{2,10},{10,18},{18,26},{... | collective-permute-start | bytes 1572872 | tf_op jit(solution)/shard_map/ppermute | solution.py:19
  160.6 3.1 fusion.44
  165.0 3.2 fusion.46
  168.2 3.3 fusion.48
  171.6 9.2 %collective-permute-done.7 = bf16[1,4,256,256]{3,2,0,1:T(8,128)(2,1)} collective-permute-done((bf16[1,4,256,256]{3,2,0,1:T(8,128)(2,1)}, bf16[1,4,256,256]{3,2,0,1:T(8,128)(2,1)}, u32[]{:S(2)}, u32[]{:S(2)}) %collective-permute-start.7) | collective-permute-done | bytes 524320 | tf_op jit(solution)/shard_map/ppermute | solution.py:22
  180.7 7.0 %fusion.25 = (f32[]{:T(128)}, f32[]{:T(128)}, f32[]{:T(128)}, f32[]{:T(128)}, f32[]{:T(128)}, /*index=5*/f32[4,2,256,256]{3,2,0,1:T(8,128)}) fusion(bf16[4,2,256,256]{3,2,0,1:T(8,128)(2,1)S(1)} %fusion.1, bf16[4,2,256,256]{3,2,0,1:T(8,128)(2,1)S(1)} %fusion.19, bf16[2,4,256,256]{3,2,1,0:T(8,128)(2,1)} %param.8, ...), kind=kOutput, calls=%fused_computation.46 | convolution fusion | flops 550502400 | bytes 13894676 | tf_op jit(solution)/shard_map/abik,blk->abil/dot_general | solution.py:32
  187.8 48.5 %all-reduce.1 = (f32[]{:T(128)}, f32[]{:T(128)}, f32[]{:T(128)}, f32[]{:T(128)}, f32[]{:T(128)}) all-reduce(f32[]{:T(128)} %get-tuple-element.9, f32[]{:T(128)} %get-tuple-element.10, f32[]{:T(128)} %get-tuple-element.8, f32[]{:T(128)} %get-tuple-element.17, f32[]{:T(128)} %get-tuple-element.11), channel_id=1, replica_groups=mesh['lsec'=4,'rsec'=8] {'lsec','rsec'}, use_global_device_ids=true, to_apply=%region_16.0 | all-reduce | flops 5 | bytes 40 | tf_op jit(solution)/shard_map/psum | solution.py:70
  241.2 2.2 fusion.24
  244.4 2.2 collective-permute-start.8
  250.8 2.2 pad_maximum_fusion.54
  253.0 5.0 %collective-permute-start.10 = (bf16[1,4,256,256]{3,2,0,1:T(8,128)(2,1)}, bf16[1,4,256,256]{3,2,0,1:T(8,128)(2,1)}, u32[]{:S(2)}, u32[]{:S(2)}) collective-permute-start(bf16[1,4,256,256]{3,2,0,1:T(8,128)(2,1)} %get-tuple-element.36), channel_id=1, source_target_pairs={{0,8},{8,16},{16,24},{1,9},{9,17},{17,25},{2,10},{10,18},{18,26},{... | collective-permute-start | bytes 1572872 | tf_op jit(solution)/shard_map/ppermute | solution.py:19
  257.9 3.0 fusion.51
  262.3 3.1 fusion.53
  265.4 3.3 fusion.55
  268.7 9.3 %collective-permute-done.11 = bf16[1,4,256,256]{3,2,0,1:T(8,128)(2,1)} collective-permute-done((bf16[1,4,256,256]{3,2,0,1:T(8,128)(2,1)}, bf16[1,4,256,256]{3,2,0,1:T(8,128)(2,1)}, u32[]{:S(2)}, u32[]{:S(2)}) %collective-permute-start.11) | collective-permute-done | bytes 524320 | tf_op jit(solution)/shard_map/ppermute | solution.py:22
  278.0 6.9 %fusion.34 = (f32[]{:T(128)}, f32[]{:T(128)}, f32[]{:T(128)}, f32[]{:T(128)}, f32[]{:T(128)}, /*index=5*/f32[4,2,256,256]{3,2,0,1:T(8,128)}) fusion(bf16[4,2,256,256]{3,2,0,1:T(8,128)(2,1)S(1)} %fusion.19, bf16[4,2,256,256]{3,2,0,1:T(8,128)(2,1)S(1)} %fusion.24, bf16[2,4,256,256]{3,2,1,0:T(8,128)(2,1)S(1)} %copy-done.2, ...), kind=kOutput, calls=%fused_computation.55 | convolution fusion | flops 550502400 | bytes 13894676 | tf_op jit(solution)/shard_map/abik,blk->abil/dot_general | solution.py:32
  284.9 49.4 %all-reduce = (f32[]{:T(128)}, f32[]{:T(128)}, f32[]{:T(128)}, f32[]{:T(128)}, f32[]{:T(128)}) all-reduce(f32[]{:T(128)} %get-tuple-element.5, f32[]{:T(128)} %get-tuple-element.6, f32[]{:T(128)} %get-tuple-element.4, f32[]{:T(128)} %get-tuple-element.18, f32[]{:T(128)} %get-tuple-element.7), channel_id=1, replica_groups=mesh['lsec'=4,'rsec'=8] {'lsec','rsec'}, use_global_device_ids=true, to_apply=%region_26.0 | all-reduce | flops 5 | bytes 40 | tf_op jit(solution)/shard_map/psum | solution.py:70
  339.7 2.1 fusion.10
  (39 shorter events, 16.3 us)
Async XLA Ops:
  47.4 13.1 %copy-start.1 = (bf16[4,4,256,256]{3,2,1,0:T(8,128)(2,1)S(1)}, bf16[4,4,256,256]{3,2,1,0:T(8,128)(2,1)}, u32[]{:S(2)}) copy-start(bf16[4,4,256,256]{3,2,1,0:T(8,128)(2,1)} %param.7) | copy-start | bytes 6291460
  47.4 2.9 collective-permute-start
  48.8 5.5 %collective-permute-start.1 = (bf16[4,1,256,256]{3,2,0,1:T(8,128)(2,1)S(1)}, bf16[4,1,256,256]{3,2,0,1:T(8,128)(2,1)S(1)}, u32[]{:S(2)}, u32[]{:S(2)}) collective-permute-start(bf16[4,1,256,256]{3,2,0,1:T(8,128)(2,1)S(1)} %get-tuple-element.46), channel_id=1, source_target_pairs={{1,0},{2,1},{3,2},{4,3},{5,4},{6,5},{7,6},{9,8},{10,9},{11,10},{12... | collective-permute-start | bytes 1572872 | tf_op jit(solution)/shard_map/ppermute | solution.py:22
  50.3 4.0 %copy-start.3 = (bf16[4,1,256,256]{3,2,0,1:T(8,128)(2,1)}, bf16[4,1,256,256]{3,2,0,1:T(8,128)(2,1)S(1)}, u32[]{:S(2)}) copy-start(bf16[4,1,256,256]{3,2,0,1:T(8,128)(2,1)S(1)} %collective-permute-done) | copy-start | bytes 1572868
  54.3 1.1 copy-start.4
  55.5 12.3 %collective-permute-start.2 = (bf16[1,4,256,256]{3,2,0,1:T(8,128)(2,1)}, bf16[1,4,256,256]{3,2,0,1:T(8,128)(2,1)}, u32[]{:S(2)}, u32[]{:S(2)}) collective-permute-start(bf16[1,4,256,256]{3,2,0,1:T(8,128)(2,1)} %get-tuple-element.40), channel_id=1, source_target_pairs={{0,8},{8,16},{16,24},{1,9},{9,17},{17,25},{2,10},{10,18},{18,26},{... | collective-permute-start | bytes 1572872 | tf_op jit(solution)/shard_map/ppermute | solution.py:19
  63.4 16.8 %collective-permute-start.3 = (bf16[1,4,256,256]{3,2,0,1:T(8,128)(2,1)}, bf16[1,4,256,256]{3,2,0,1:T(8,128)(2,1)}, u32[]{:S(2)}, u32[]{:S(2)}) collective-permute-start(bf16[1,4,256,256]{3,2,0,1:T(8,128)(2,1)} %get-tuple-element.39), channel_id=1, source_target_pairs={{8,0},{16,8},{24,16},{9,1},{17,9},{25,17},{10,2},{18,10},{26,18},{... | collective-permute-start | bytes 1572872 | tf_op jit(solution)/shard_map/ppermute | solution.py:22
  67.7 12.5 %copy-start.7 = (f32[4,2]{0,1:T(2,128)S(1)}, f32[4,2]{0,1:T(2,128)}, u32[]{:S(2)}) copy-start(f32[4,2]{0,1:T(2,128)} %param.9) | copy-start | bytes 100
  71.0 72.9 %copy-start = (bf16[4,2,256,256]{3,2,1,0:T(8,128)(2,1)S(1)}, bf16[4,2,256,256]{3,2,1,0:T(8,128)(2,1)}, u32[]{:S(2)}) copy-start(bf16[4,2,256,256]{3,2,1,0:T(8,128)(2,1)} %param.6) | copy-start | bytes 3145732
  145.8 4.5 %copy-start.5 = (s32[2]{0:T(128)S(1)}, s32[2]{0:T(128)}, u32[]{:S(2)}) copy-start(s32[2]{0:T(128)} %param.10) | copy-start | bytes 28
  145.8 5.7 %copy-start.6 = (s32[2]{0:T(128)S(1)}, s32[2]{0:T(128)}, u32[]{:S(2)}) copy-start(s32[2]{0:T(128)} %param.11) | copy-start | bytes 28
  146.9 6.6 %collective-permute-start.4 = (bf16[4,1,256,256]{3,2,0,1:T(8,128)(2,1)}, bf16[4,1,256,256]{3,2,0,1:T(8,128)(2,1)}, u32[]{:S(2)}, u32[]{:S(2)}) collective-permute-start(bf16[4,1,256,256]{3,2,0,1:T(8,128)(2,1)} %get-tuple-element.43), channel_id=1, source_target_pairs={{0,1},{1,2},{2,3},{3,4},{4,5},{5,6},{6,7},{8,9},{9,10},{10,11},{11... | collective-permute-start | bytes 1572872 | tf_op jit(solution)/shard_map/ppermute | solution.py:19
  149.0 4.5 %collective-permute-start.5 = (bf16[4,1,256,256]{3,2,0,1:T(8,128)(2,1)}, bf16[4,1,256,256]{3,2,0,1:T(8,128)(2,1)}, u32[]{:S(2)}, u32[]{:S(2)}) collective-permute-start(bf16[4,1,256,256]{3,2,0,1:T(8,128)(2,1)} %get-tuple-element.44), channel_id=1, source_target_pairs={{1,0},{2,1},{3,2},{4,3},{5,4},{6,5},{7,6},{9,8},{10,9},{11,10},{12... | collective-permute-start | bytes 1572872 | tf_op jit(solution)/shard_map/ppermute | solution.py:22
  155.6 12.6 %collective-permute-start.6 = (bf16[1,4,256,256]{3,2,0,1:T(8,128)(2,1)}, bf16[1,4,256,256]{3,2,0,1:T(8,128)(2,1)}, u32[]{:S(2)}, u32[]{:S(2)}) collective-permute-start(bf16[1,4,256,256]{3,2,0,1:T(8,128)(2,1)} %get-tuple-element.38), channel_id=1, source_target_pairs={{0,8},{8,16},{16,24},{1,9},{9,17},{17,25},{2,10},{10,18},{18,26},{... | collective-permute-start | bytes 1572872 | tf_op jit(solution)/shard_map/ppermute | solution.py:19
  163.8 17.0 %collective-permute-start.7 = (bf16[1,4,256,256]{3,2,0,1:T(8,128)(2,1)}, bf16[1,4,256,256]{3,2,0,1:T(8,128)(2,1)}, u32[]{:S(2)}, u32[]{:S(2)}) collective-permute-start(bf16[1,4,256,256]{3,2,0,1:T(8,128)(2,1)} %get-tuple-element.37), channel_id=1, source_target_pairs={{8,0},{16,8},{24,16},{9,1},{17,9},{25,17},{10,2},{18,10},{26,18},{... | collective-permute-start | bytes 1572872 | tf_op jit(solution)/shard_map/ppermute | solution.py:22
  244.4 13.5 %copy-start.2 = (bf16[2,4,256,256]{3,2,1,0:T(8,128)(2,1)S(1)}, bf16[2,4,256,256]{3,2,1,0:T(8,128)(2,1)}, u32[]{:S(2)}) copy-start(bf16[2,4,256,256]{3,2,1,0:T(8,128)(2,1)} %param.8) | copy-start | bytes 3145732
  244.4 5.5 %collective-permute-start.8 = (bf16[4,1,256,256]{3,2,0,1:T(8,128)(2,1)}, bf16[4,1,256,256]{3,2,0,1:T(8,128)(2,1)}, u32[]{:S(2)}, u32[]{:S(2)}) collective-permute-start(bf16[4,1,256,256]{3,2,0,1:T(8,128)(2,1)} %get-tuple-element.41), channel_id=1, source_target_pairs={{0,1},{1,2},{2,3},{3,4},{4,5},{5,6},{6,7},{8,9},{9,10},{10,11},{11... | collective-permute-start | bytes 1572872 | tf_op jit(solution)/shard_map/ppermute | solution.py:19
  246.6 4.1 %collective-permute-start.9 = (bf16[4,1,256,256]{3,2,0,1:T(8,128)(2,1)}, bf16[4,1,256,256]{3,2,0,1:T(8,128)(2,1)}, u32[]{:S(2)}, u32[]{:S(2)}) collective-permute-start(bf16[4,1,256,256]{3,2,0,1:T(8,128)(2,1)} %get-tuple-element.42), channel_id=1, source_target_pairs={{1,0},{2,1},{3,2},{4,3},{5,4},{6,5},{7,6},{9,8},{10,9},{11,10},{12... | collective-permute-start | bytes 1572872 | tf_op jit(solution)/shard_map/ppermute | solution.py:22
  253.0 12.4 %collective-permute-start.10 = (bf16[1,4,256,256]{3,2,0,1:T(8,128)(2,1)}, bf16[1,4,256,256]{3,2,0,1:T(8,128)(2,1)}, u32[]{:S(2)}, u32[]{:S(2)}) collective-permute-start(bf16[1,4,256,256]{3,2,0,1:T(8,128)(2,1)} %get-tuple-element.36), channel_id=1, source_target_pairs={{0,8},{8,16},{16,24},{1,9},{9,17},{17,25},{2,10},{10,18},{18,26},{... | collective-permute-start | bytes 1572872 | tf_op jit(solution)/shard_map/ppermute | solution.py:19
  261.0 17.0 %collective-permute-start.11 = (bf16[1,4,256,256]{3,2,0,1:T(8,128)(2,1)}, bf16[1,4,256,256]{3,2,0,1:T(8,128)(2,1)}, u32[]{:S(2)}, u32[]{:S(2)}) collective-permute-start(bf16[1,4,256,256]{3,2,0,1:T(8,128)(2,1)} %get-tuple-element.35), channel_id=1, source_target_pairs={{8,0},{16,8},{24,16},{9,1},{17,9},{25,17},{10,2},{18,10},{26,18},{... | collective-permute-start | bytes 1572872 | tf_op jit(solution)/shard_map/ppermute | solution.py:22
where the time goes:
time: 345 us; the launch traced here: 343 us
  blocking collectives  191 us (55%)
  matrix products  49.2 us (14%)
  waiting for transfers between devices  32.9 us (10%)
  starting transfers between devices  28.5 us (8%)
  between operations  21.7 us (6%)
  other arithmetic  16.1 us (5%)
  local copies, waits for them, and re-layouts  4.39 us (1%)
    psum x3, blocking collectives, per_device(): lax.psum((jnp.sum(sigma * sigma), jnp.sum(sigma * vals), jnp.sum(sigma *...  149 us
    dot_general x12, matrix products, add_terms(): jnp.einsum('abik,blk->abil', inner, right_env[:, term], preferred_element...  49.2 us
    psum x1, blocking collectives, per_device(): start = lax.psum(jnp.sum(start_vals * start_vals), ('lsec', 'rsec')) * count  42.2 us
    ppermute x6, waiting for transfers between devices, padded(): lax.ppermute(lax.slice_in_dim(block, 0, width, axis=dim), axis, backward)  32.7 us
    ppermute x6, starting transfers between devices, padded(): lax.ppermute(lax.slice_in_dim(block, block.shape[dim] - width, None, axis...  20.8 us
    ppermute x6, starting transfers between devices, padded(): lax.ppermute(lax.slice_in_dim(block, 0, width, axis=dim), axis, backward)  7.69 us
  transfers between devices with their start and end apart: 12, of which 6 were waited for; matrix products, arithmetic and copies ran while one was open for 9% of the time, Pallas kernels for 0%

commit v1 on v0

v1 whole, which is shorter than its diff:
```python
import functools

import jax
import jax.numpy as jnp
from jax import lax
from jax.experimental import pallas as pl
from jax.experimental.pallas import tpu as pltpu
from jax.sharding import PartitionSpec as P

DIAG = 2
HOPS = 1
TERMS = DIAG + 2 * HOPS
ITERS = 3
eps = 1e-06
SHIFT = 1.75
GRAMS = 16
MESH = pl.DeviceIdType.MESH


def gram_row(i, j):
    return j * (j + 1) // 2 + i


def kernel(
    nl, nr, count,
    psi_hbm, left_hbm, right_hbm, energies, coef_num, coef_den,
    out_hbm, ritz,
    q, left, right, right_t, acc, out_v, rows, cols,
    send_sem, recv_sem, in_sem, rsend, rrecv, csend, crecv,
):
    na, nb, size, _ = psi_hbm.shape
    me_l, me_r = lax.axis_index("lsec"), lax.axis_index("rsec")
    has_lo_l, has_hi_l = me_l > 0, me_l < nl - 1
    has_lo_r, has_hi_r = me_r > 0, me_r < nr - 1
    up_dn = jnp.logical_and(has_hi_l, has_lo_r)
    dn_up = jnp.logical_and(has_lo_l, has_hi_r)

    loads = [
        pltpu.make_async_copy(psi_hbm, q.at[0, 1 : na + 1, 1 : nb + 1], in_sem.at[0]),
        pltpu.make_async_copy(right_hbm, right, in_sem.at[1]),
        pltpu.make_async_copy(left_hbm, left, in_sem.at[2]),
    ]
    for load in loads:
        load.start()

    barrier = pltpu.get_barrier_semaphore()

    def greet(target):
        pl.semaphore_signal(barrier, inc=1, device_id=target, device_id_type=MESH)

    for step in range(1, nr):
        greet((me_l, lax.rem(me_r + step, nr)))
    for step in range(1, nl):
        greet((lax.rem(me_l + step, nl), me_r))

    @pl.when(up_dn)
    def _():
        greet((me_l + 1, me_r - 1))

    @pl.when(dn_up)
    def _():
        greet((me_l - 1, me_r + 1))

    def hops(k):
        lo_l, hi_l, lo_r, hi_r = me_l - 1, me_l + 1, me_r - 1, me_r + 1
        here = q.at[k]
        plan = (
            (has_hi_l, has_lo_l, here.at[na, 2 : nb + 1], here.at[0, 2 : nb + 1], (hi_l, me_r)),
            (up_dn, dn_up, here.at[na, 1], here.at[0, nb + 1], (hi_l, lo_r)),
            (has_lo_l, has_hi_l, here.at[1, 1:nb], here.at[na + 1, 1:nb], (lo_l, me_r)),
            (dn_up, up_dn, here.at[1, nb], here.at[na + 1, 0], (lo_l, hi_r)),
            (has_lo_r, has_hi_r, here.at[1:na, 1], here.at[1:na, nb + 1], (me_l, lo_r)),
            (has_hi_r, has_lo_r, here.at[2 : na + 1, nb], here.at[2 : na + 1, 0], (me_l, hi_r)),
        )

        def copy(n):
            return pltpu.make_async_remote_copy(
                src_ref=plan[n][2], dst_ref=plan[n][3],
                send_sem=send_sem.at[k, n], recv_sem=recv_sem.at[k, n],
                device_id=plan[n][4], device_id_type=MESH,
            )

        return plan, copy

    def send(k, which):
        plan, copy = hops(k)
        for n in which:
            pl.when(plan[n][0])(lambda n=n: copy(n).start())

    def receive(k, which):
        plan, copy = hops(k)
        for n in which:
            pl.when(plan[n][1])(lambda n=n: copy(n).wait_recv())

    def clear(missing, slots):
        @pl.when(jnp.logical_not(missing))
        def _():
            for k in range(ITERS):
                for i, j in slots:
                    q[k, i, j] = jnp.zeros((size, size), q.dtype)

    clear(has_lo_l, [(0, j) for j in range(2, nb + 1)])
    clear(dn_up, [(0, nb + 1)])
    clear(has_hi_l, [(na + 1, j) for j in range(1, nb)])
    clear(up_dn, [(na + 1, 0)])
    clear(has_hi_r, [(i, nb + 1) for i in range(1, na)])
    clear(has_lo_r, [(i, 0) for i in range(2, na + 1)])

    rows[me_r] = jnp.zeros(rows.shape[1:], jnp.float32)
    partners = nr - 1 + nl - 1
    partners = partners + up_dn.astype(jnp.int32) + dn_up.astype(jnp.int32)
    loads[0].wait()
    pl.semaphore_wait(barrier, partners)
    send(0, range(6))
    loads[1].wait()
    for j in range(nb):
        for t in range(TERMS):
            right_t[j, t] = right[j, t].T
    loads[2].wait()

    def term(i, j, t, source):
        inner = jnp.dot(left[i, t], source, preferred_element_type=jnp.float32)
        return jnp.dot(
            inner.astype(jnp.bfloat16), right_t[j, t], preferred_element_type=jnp.float32
        )

    def gram(i, j):
        total = jnp.zeros((size, size), jnp.float32)
        for a in range(1, na + 1):
            for b in range(1, nb + 1):
                total += q[i, a, b].astype(jnp.float32) * q[j, a, b].astype(jnp.float32)
        folded = jnp.sum(total, axis=0, keepdims=True)
        part = folded[:, 0:128]
        for lane in range(128, size, 128):
            part = part + folded[:, lane : lane + 128]
        rows[me_r, pl.ds(gram_row(i, j), 1), :] = part

    gram(0, 0)

    def is_local(t, i, j):
        if t < DIAG:
            return True
        if t < DIAG + HOPS:
            return i >= 1 and j + 1 < nb
        return i + 1 < na and j >= 1

    def offset(t):
        return 0 if t < DIAG else (1 if t < DIAG + HOPS else -1)

    def source_of(k, t, i, j):
        return q[k, i + 1 - offset(t), j + 1 + offset(t)]

    def step(k, carry):
        for i in range(na):
            for j in range(nb):
                own = q[k, i + 1, j + 1]
                total = (energies[i, j] - SHIFT) * own.astype(jnp.float32)
                for t in range(TERMS):
                    if is_local(t, i, j):
                        total += term(i, j, t, source_of(k, t, i, j))
                acc[i, j] = total

        def finish(i, j, ts):
            total = acc[i, j]
            for t in ts:
                total += term(i, j, t, source_of(k, t, i, j))
            acc[i, j] = total
            q[k + 1, i + 1, j + 1] = total.astype(jnp.bfloat16)

        corners = ((0, 0), (na - 1, nb - 1), (0, nb - 1), (na - 1, 0))
        receive(k, (5, 4))
        for i in range(na):
            for j in range(nb):
                if (i, j) not in corners:
                    finish(i, j, [t for t in range(DIAG, TERMS) if not is_local(t, i, j)])
        receive(k, (0, 2, 1, 3))
        for i, j in corners:
            finish(i, j, [t for t in range(DIAG, TERMS) if not is_local(t, i, j)])

        @pl.when(k + 1 < ITERS)
        def _():
            send(k + 1, range(6))

        lax.fori_loop(0, k + 2, lambda i, c: (gram(i, k + 1), c)[1], 0)
        return carry

    lax.fori_loop(0, ITERS, step, 0)

    def spread(slots, me, parts, to, ssem, rsem):
        def copy(n, slot):
            return pltpu.make_async_remote_copy(
                src_ref=slots.at[slot], dst_ref=slots.at[slot],
                send_sem=ssem.at[n], recv_sem=rsem.at[slot],
                device_id=to(lax.rem(me + n, parts)), device_id_type=MESH,
            )

        for n in range(1, parts):
            copy(n, me).start()
        for n in range(1, parts):
            copy(n, lax.rem(me + n, parts)).wait_recv()
        for n in range(1, parts):
            copy(n, me).wait_send()
        total = slots[0]
        for n in range(1, parts):
            total = total + slots[n]
        return total

    cols[me_l] = spread(rows, me_r, nr, lambda r: (me_l, r), rsend, rrecv)
    sums = spread(cols, me_l, nl, lambda l: (l, me_r), csend, crecv)
    sums = jnp.sum(sums, axis=1, keepdims=True) * count

    def mean(i, j):
        row = gram_row(min(i, j), max(i, j))
        return sums[row : row + 1, :]

    def product(x, y):
        total = jnp.zeros((1, 1), jnp.float32)
        for i in range(ITERS + 1):
            for j in range(ITERS + 1):
                if x[i] is not None and y[j] is not None:
                    total = total + x[i] * y[j] * mean(i, j)
        return total

    def plus(x, y):
        return y if x is None else (x if y is None else x + y)

    def scaled(s, x):
        return [None if part is None else s * part for part in x]

    def combine(*lists):
        return [functools.reduce(plus, parts) for parts in zip(*lists)]

    vec = [lax.rsqrt(mean(0, 0) + eps)] + [None] * ITERS
    previous = [None] * (ITERS + 1)
    for k in range(ITERS):
        sigma = combine([None] + vec[:-1], scaled(SHIFT, vec))
        theta = product(vec, sigma)
        resid = combine(sigma, scaled(-theta, vec))
        if k > 0:
            coef = jnp.full((1, 1), coef_num[k - 1].astype(jnp.float32)) / jnp.full(
                (1, 1), coef_den[k - 1].astype(jnp.float32)
            )
            resid = combine(resid, scaled(-coef, previous))
        ritz[k] = theta[0, 0]
        previous = vec
        vec = scaled(lax.rsqrt(product(resid, resid) + eps), resid)

    stores = []
    for i in range(na):
        for j in range(nb):
            total = acc[i, j] * vec[ITERS]
            for n in range(ITERS):
                total += q[n, i + 1, j + 1].astype(jnp.float32) * vec[n]
            out_v[i, j] = total.astype(jnp.bfloat16)
        stores.append(pltpu.make_async_copy(out_v.at[i], out_hbm.at[i], in_sem.at[i]))
        stores[-1].start()

    for k in range(ITERS):
        plan, copy = hops(k)
        for n in range(6):
            pl.when(plan[n][0])(lambda n=n: copy(n).wait_send())
    for store in stores:
        store.wait()


def per_device(nl, nr, psi, left_env, right_env, energies, coef_num, coef_den):
    na, nb, size, _ = psi.shape
    count = 1.0 / float(psi.size * nl * nr)
    anywhere = pl.BlockSpec(memory_space=pl.ANY)
    smem = pl.BlockSpec(memory_space=pltpu.SMEM)
    dma = pltpu.SemaphoreType.DMA
    return pl.pallas_call(
        functools.partial(kernel, nl, nr, count),
        out_shape=(
            jax.ShapeDtypeStruct(psi.shape, jnp.bfloat16),
            jax.ShapeDtypeStruct((ITERS,), jnp.float32),
        ),
        in_specs=[anywhere] * 3 + [smem] * 3,
        out_specs=(anywhere, smem),
        scratch_shapes=[
            pltpu.VMEM((ITERS + 1, na + 2, nb + 2, size, size), jnp.bfloat16),
            pltpu.VMEM(left_env.shape, jnp.bfloat16),
            pltpu.VMEM(right_env.shape, jnp.bfloat16),
            pltpu.VMEM(right_env.shape, jnp.bfloat16),
            pltpu.VMEM(psi.shape, jnp.float32),
            pltpu.VMEM(psi.shape, jnp.bfloat16),
            pltpu.VMEM((nr, GRAMS, 128), jnp.float32),
            pltpu.VMEM((nl, GRAMS, 128), jnp.float32),
            dma((ITERS, 6)),
            dma((ITERS, 6)),
            dma((max(3, na),)),
            dma((nr,)),
            dma((nr,)),
            dma((nl,)),
            dma((nl,)),
        ],
        compiler_params=pltpu.CompilerParams(
            collective_id=0, has_side_effects=True, vmem_limit_bytes=60000000
        ),
    )(psi, left_env, right_env, energies, coef_num, coef_den)


def solution(mesh):
    in_specs = (
        P("lsec", "rsec", None, None),
        P("lsec", None, None, None),
        P("rsec", None, None, None),
        P("lsec", "rsec"),
        P(),
        P(),
    )
    out_specs = (P("lsec", "rsec", None, None), P())
    body = functools.partial(per_device, mesh.shape["lsec"], mesh.shape["rsec"])
    return jax.shard_map(
        body, mesh=mesh, in_specs=in_specs, out_specs=out_specs, check_vma=False
    )
```

time: 345 us -> 58.7 us (0.17)
  blocking collectives: 191 us -> 0 us
  Pallas kernels: 0 us -> 53.7 us
  matrix products: 49.2 us -> 0 us
  waiting for transfers between devices: 32.9 us -> 0 us
  starting transfers between devices: 28.5 us -> 0 us
  between operations: 21.7 us -> 0.65 us
  other arithmetic: 16.1 us -> 0 us
    psum x4 -> x0, blocking collectives: 191 us -> none  [the longest x3 149 us: per_device(): lax.psum((jnp.sum(sigma * sigma), jnp.sum(sigma * vals), jnp.sum(sigma *...]
    pallas_call x0 -> x1, Pallas kernels: none -> 53.7 us  [per_device(): pl.pallas_call(functools.partial(kernel, nl, nr, count), out_shape=(jax.S...]
    dot_general x12 -> x0, matrix products: 49.2 us -> none  [add_terms(): jnp.einsum('abik,blk->abil', inner, right_env[:, term], preferred_element...]
    ppermute x12 -> x0, waiting for transfers between devices: 32.9 us -> none  [the longest x6 32.7 us: padded(): lax.ppermute(lax.slice_in_dim(block, 0, width, axis=dim), axis, backward)]
    ppermute x12 -> x0, starting transfers between devices: 28.5 us -> none  [the longest x6 20.8 us: padded(): lax.ppermute(lax.slice_in_dim(block, block.shape[dim] - width, None, axis...]
    convert_element_type x4 -> x0, other arithmetic: 7.67 us -> none  [the longest x3 6.25 us: per_device(): vec = (resid * lax.rsqrt(norm_sq + eps)).astype(jnp.bfloat16)]
    concatenate x3 -> x0, other arithmetic: 5.5 us -> none  [padded(): block = jnp.concatenate([low, block, high], axis=dim)]
  transfers between devices with their start and end apart: 12 -> 0, of which waited for: 6 -> 0; matrix products, arithmetic and copies ran while one was open for 9% -> 0% of each run, Pallas kernels for 0% -> 0%
where the time goes in v1:
time: 58.7 us; the launch traced here: 58.5 us
  Pallas kernels  53.7 us (91%)
  local copies, waits for them, and re-layouts  4.11 us (7%)
  between operations  0.65 us (1%)
    pallas_call x1, Pallas kernels, per_device(): pl.pallas_call(functools.partial(kernel, nl, nr, count), out_shape=(jax.S...  53.7 us
    unnamed x5, local copies, waits for them, and re-layouts  4.11 us

profile of v1, /device:TPU:0, one launch (start us, length us, event | category | flops | bytes accessed | tf_op | source)
XLA Modules:
  0.0 58.5 jit_solution(12944843293128235990)
XLA Ops:
  0.6 1.3 %copy.8.energies = f32[4,2]{1,0:T(4,128)} copy(f32[4,2]{0,1:T(2,128)} %param.9) | data formatting | bytes 64 | tf_op args[3]
  2.0 53.7 %shard_map.77 = (bf16[4,2,256,256]{3,2,1,0:T(8,128)(2,1)}, f32[3]{0:T(128)}) custom-call(bf16[4,2,256,256]{3,2,1,0:T(8,128)(2,1)} %psi_hbm.1, bf16[4,4,256,256]{3,2,1,0:T(8,128)(2,1)} %left_hbm.1, bf16[2,4,256,256]{3,2,1,0:T(8,128)(2,1)} %right_hbm.1, f32[4,2]{1,0:T(4,128)} %copy.8.energies, s32[2]{0:T(128)} %coef_num.1, s32[2]{0:T(128)} %coef_den.1), custom_call_target="tpu_custom_call" | custom-call | tf_op jit(solution)/shard_map/pallas_call | solution.py:272
  55.7 0.0 copy-start
  55.7 2.3 %copy.11 = bf16[4,2,256,256]{3,2,1,0:T(8,128)(2,1)} copy(bf16[4,2,256,256]{3,2,1,0:T(8,128)(2,1)} %get-tuple-element.4) | data formatting | bytes 2097152
  58.0 0.0 copy-done
  58.0 0.5 copy.12
Async XLA Ops:
  55.7 2.3 %copy-start = (f32[3]{0:T(128)S(1)}, f32[3]{0:T(128)}, u32[]{:S(2)}) copy-start(f32[3]{0:T(128)} %get-tuple-element.5) | copy-start | bytes 40

commit v2 on v1

--- a/solution.py
+++ b/solution.py
@@ -25,7 +25,7 @@
     nl, nr, count,
     psi_hbm, left_hbm, right_hbm, energies, coef_num, coef_den,
     out_hbm, ritz,
-    q, left, right, right_t, acc, out_v, rows, cols,
+    q, stage, left, right, right_t, acc, out_v, rows, cols,
     send_sem, recv_sem, in_sem, rsend, rrecv, csend, crecv,
 ):
     na, nb, size, _ = psi_hbm.shape
@@ -34,6 +34,14 @@
     has_lo_r, has_hi_r = me_r > 0, me_r < nr - 1
     up_dn = jnp.logical_and(has_hi_l, has_lo_r)
     dn_up = jnp.logical_and(has_lo_l, has_hi_r)
+    odd = lax.rem(me_l, 2) == 1
+    even = jnp.logical_not(odd)
+    via_hi = jnp.logical_and(up_dn, jnp.logical_and(odd, me_l + 2 < nl))
+    via_lo = jnp.logical_and(dn_up, jnp.logical_and(even, me_l >= 2))
+    relay_dn = jnp.logical_and(jnp.logical_and(odd, me_l >= 2), has_lo_r)
+    relay_up = jnp.logical_and(jnp.logical_and(even, me_l + 2 < nl), has_hi_r)
+    up_up = jnp.logical_and(even, jnp.logical_and(has_hi_l, has_hi_r))
+    dn_dn = jnp.logical_and(odd, has_lo_r)
 
     loads = [
         pltpu.make_async_copy(psi_hbm, q.at[0, 1 : na + 1, 1 : nb + 1], in_sem.at[0]),
@@ -61,36 +69,55 @@
     def _():
         greet((me_l - 1, me_r + 1))
 
+    @pl.when(up_up)
+    def _():
+        greet((me_l + 1, me_r + 1))
+
+    @pl.when(dn_dn)
+    def _():
+        greet((me_l - 1, me_r - 1))
+
     def hops(k):
         lo_l, hi_l, lo_r, hi_r = me_l - 1, me_l + 1, me_r - 1, me_r + 1
         here = q.at[k]
-        plan = (
-            (has_hi_l, has_lo_l, here.at[na, 2 : nb + 1], here.at[0, 2 : nb + 1], (hi_l, me_r)),
-            (up_dn, dn_up, here.at[na, 1], here.at[0, nb + 1], (hi_l, lo_r)),
-            (has_lo_l, has_hi_l, here.at[1, 1:nb], here.at[na + 1, 1:nb], (lo_l, me_r)),
-            (dn_up, up_dn, here.at[1, nb], here.at[na + 1, 0], (lo_l, hi_r)),
-            (has_lo_r, has_hi_r, here.at[1:na, 1], here.at[1:na, nb + 1], (me_l, lo_r)),
-            (has_hi_r, has_lo_r, here.at[2 : na + 1, nb], here.at[2 : na + 1, 0], (me_l, hi_r)),
+        up_ref, dn_ref = here.at[na, 1], here.at[1, nb]
+        up_dst, dn_dst = here.at[0, nb + 1], here.at[na + 1, 0]
+        up_stage, dn_stage = stage.at[k, 0], stage.at[k, 1]
+        no = jnp.logical_not
+        return (
+            (has_hi_l, has_lo_l, here.at[na, 2 : nb + 1], here.at[0, 2 : nb + 1], (hi_l, me_r), 0, 0),
+            (jnp.logical_and(up_dn, no(via_hi)), dn_up, up_ref, up_dst, (hi_l, lo_r), 1, 1),
+            (has_lo_l, has_hi_l, here.at[1, 1:nb], here.at[na + 1, 1:nb], (lo_l, me_r), 2, 2),
+            (jnp.logical_and(dn_up, no(via_lo)), up_dn, dn_ref, dn_dst, (lo_l, hi_r), 3, 3),
+            (has_lo_r, has_hi_r, here.at[2:na, 1], here.at[2:na, nb + 1], (me_l, lo_r), 4, 4),
+            (has_hi_r, has_lo_r, here.at[2:na, nb], here.at[2:na, 0], (me_l, hi_r), 5, 5),
+            (has_lo_r, has_hi_r, here.at[1, 1], here.at[1, nb + 1], (me_l, lo_r), 6, 6),
+            (has_hi_r, has_lo_r, here.at[na, nb], here.at[na, 0], (me_l, hi_r), 7, 7),
+            (via_hi, relay_dn, up_ref, up_stage, (me_l + 2, me_r), 1, 8),
+            (via_lo, relay_up, dn_ref, dn_stage, (me_l - 2, me_r), 3, 9),
+            (relay_dn, None, up_stage, up_dst, (lo_l, lo_r), 8, 1),
+            (relay_up, None, dn_stage, dn_dst, (hi_l, hi_r), 9, 3),
         )
 
-        def copy(n):
-            return pltpu.make_async_remote_copy(
-                src_ref=plan[n][2], dst_ref=plan[n][3],
-                send_sem=send_sem.at[k, n], recv_sem=recv_sem.at[k, n],
-                device_id=plan[n][4], device_id_type=MESH,
-            )
-
-        return plan, copy
+    def copy(k, n):
+        _, _, src, dst, target, ssem, rsem = hops(k)[n]
+        return pltpu.make_async_remote_copy(
+            src_ref=src, dst_ref=dst,
+            send_sem=send_sem.at[k, ssem], recv_sem=recv_sem.at[k, rsem],
+            device_id=target, device_id_type=MESH,
+        )
 
     def send(k, which):
-        plan, copy = hops(k)
         for n in which:
-            pl.when(plan[n][0])(lambda n=n: copy(n).start())
+            pl.when(hops(k)[n][0])(lambda n=n: copy(k, n).start())
 
     def receive(k, which):
-        plan, copy = hops(k)
         for n in which:
-            pl.when(plan[n][1])(lambda n=n: copy(n).wait_recv())
+            pl.when(hops(k)[n][1])(lambda n=n: copy(k, n).wait_recv())
+
+    def forward(k):
+        receive(k, (8, 9))
+        send(k, (10, 11))
 
     def clear(missing, slots):
         @pl.when(jnp.logical_not(missing))
@@ -108,10 +135,11 @@
 
     rows[me_r] = jnp.zeros(rows.shape[1:], jnp.float32)
     partners = nr - 1 + nl - 1
-    partners = partners + up_dn.astype(jnp.int32) + dn_up.astype(jnp.int32)
+    for other in (up_dn, dn_up, up_up, dn_dn):
+        partners = partners + other.astype(jnp.int32)
     loads[0].wait()
     pl.semaphore_wait(barrier, partners)
-    send(0, range(6))
+    send(0, (8, 9, 0, 2, 1, 3, 4, 5, 6, 7))
     loads[1].wait()
     for j in range(nb):
         for t in range(TERMS):
@@ -154,7 +182,7 @@
         for i in range(na):
             for j in range(nb):
                 own = q[k, i + 1, j + 1]
-                total = (energies[i, j] - SHIFT) * own.astype(jnp.float32)
+                total = (energies[j, i] - SHIFT) * own.astype(jnp.float32)
                 for t in range(TERMS):
                     if is_local(t, i, j):
                         total += term(i, j, t, source_of(k, t, i, j))
@@ -167,19 +195,32 @@
             acc[i, j] = total
             q[k + 1, i + 1, j + 1] = total.astype(jnp.bfloat16)
 
-        corners = ((0, 0), (na - 1, nb - 1), (0, nb - 1), (na - 1, 0))
-        receive(k, (5, 4))
-        for i in range(na):
+        def remote(i, j):
+            return [t for t in range(DIAG, TERMS) if not is_local(t, i, j)]
+
+        def onward(which):
+            pl.when(k + 1 < ITERS)(lambda: send(k + 1, which))
+
+        forward(k)
+        receive(k, (4, 5, 6, 7))
+        for i in range(1, na - 1):
             for j in range(nb):
-                if (i, j) not in corners:
-                    finish(i, j, [t for t in range(DIAG, TERMS) if not is_local(t, i, j)])
-        receive(k, (0, 2, 1, 3))
-        for i, j in corners:
-            finish(i, j, [t for t in range(DIAG, TERMS) if not is_local(t, i, j)])
-
-        @pl.when(k + 1 < ITERS)
-        def _():
-            send(k + 1, range(6))
+                finish(i, j, remote(i, j))
+        onward((4, 5))
+        receive(k, (0,))
+        for j in range(nb - 1):
+            finish(0, j, remote(0, j))
+        onward((2, 6))
+        receive(k, (2,))
+        for j in range(1, nb):
+            finish(na - 1, j, remote(na - 1, j))
+        onward((0, 7))
+        receive(k, (1,))
+        finish(0, nb - 1, remote(0, nb - 1))
+        onward((9, 3))
+        receive(k, (3,))
+        finish(na - 1, 0, remote(na - 1, 0))
+        onward((8, 1))
 
         lax.fori_loop(0, k + 2, lambda i, c: (gram(i, k + 1), c)[1], 0)
         return carry
@@ -256,9 +297,8 @@
         stores[-1].start()
 
     for k in range(ITERS):
-        plan, copy = hops(k)
-        for n in range(6):
-            pl.when(plan[n][0])(lambda n=n: copy(n).wait_send())
+        for n in range(12):
+            pl.when(hops(k)[n][0])(lambda k=k, n=n: copy(k, n).wait_send())
     for store in stores:
         store.wait()
 
@@ -279,6 +319,7 @@
         out_specs=(anywhere, smem),
         scratch_shapes=[
             pltpu.VMEM((ITERS + 1, na + 2, nb + 2, size, size), jnp.bfloat16),
+            pltpu.VMEM((ITERS, 2, size, size), jnp.bfloat16),
             pltpu.VMEM(left_env.shape, jnp.bfloat16),
             pltpu.VMEM(right_env.shape, jnp.bfloat16),
             pltpu.VMEM(right_env.shape, jnp.bfloat16),
@@ -286,8 +327,8 @@
             pltpu.VMEM(psi.shape, jnp.bfloat16),
             pltpu.VMEM((nr, GRAMS, 128), jnp.float32),
             pltpu.VMEM((nl, GRAMS, 128), jnp.float32),
-            dma((ITERS, 6)),
-            dma((ITERS, 6)),
+            dma((ITERS, 10)),
+            dma((ITERS, 10)),
             dma((max(3, na),)),
             dma((nr,)),
             dma((nr,)),
@@ -297,7 +338,7 @@
         compiler_params=pltpu.CompilerParams(
             collective_id=0, has_side_effects=True, vmem_limit_bytes=60000000
         ),
-    )(psi, left_env, right_env, energies, coef_num, coef_den)
+    )(psi, left_env, right_env, energies.T, coef_num, coef_den)
 
 
 def solution(mesh):

time: 58.7 us -> 49.8 us (0.85)
  Pallas kernels: 53.7 us -> 46.2 us
  local copies, waits for them, and re-layouts: 4.11 us -> 2.78 us
    pallas_call x1, Pallas kernels: 53.7 us -> 46.2 us  [per_device(): pl.pallas_call(functools.partial(kernel, nl, nr, count), out_shape=(jax.S...]
    unnamed x5 -> x4, local copies, waits for them, and re-layouts: 4.11 us -> 2.78 us
where the time goes in v2:
time: 49.8 us; the launch traced here: 49.6 us
  Pallas kernels  46.2 us (93%)
  local copies, waits for them, and re-layouts  2.78 us (6%)
  between operations  0.65 us (1%)
    pallas_call x1, Pallas kernels, per_device(): pl.pallas_call(functools.partial(kernel, nl, nr, count), out_shape=(jax.S...  46.2 us
    unnamed x4, local copies, waits for them, and re-layouts  2.78 us

profile of v2, /device:TPU:0, one launch (start us, length us, event | category | flops | bytes accessed | tf_op | source)
XLA Modules:
  0.0 49.6 jit_solution(146146129785586291)
XLA Ops:
  0.6 46.2 %shard_map.77 = (bf16[4,2,256,256]{3,2,1,0:T(8,128)(2,1)}, f32[3]{0:T(128)}) custom-call(bf16[4,2,256,256]{3,2,1,0:T(8,128)(2,1)} %psi_hbm.1, bf16[4,4,256,256]{3,2,1,0:T(8,128)(2,1)} %left_hbm.1, bf16[2,4,256,256]{3,2,1,0:T(8,128)(2,1)} %right_hbm.1, f32[2,4]{1,0:T(2,128)} %bitcast.1, s32[2]{0:T(128)} %coef_num.1, s32[2]{0:T(128)} %coef_den.1), custom_call_target="tpu_custom_call" | custom-call | tf_op jit(solution)/shard_map/pallas_call | solution.py:312
  46.8 0.0 copy-start
  46.9 2.3 %copy.10 = bf16[4,2,256,256]{3,2,1,0:T(8,128)(2,1)} copy(bf16[4,2,256,256]{3,2,1,0:T(8,128)(2,1)} %get-tuple-element.4) | data formatting | bytes 2097152
  49.1 0.0 copy-done
  49.1 0.5 %copy.11 = f32[3]{0:T(128)} copy(f32[3]{0:T(128)S(1)} %copy-done) | data formatting | bytes 24
Async XLA Ops:
  46.8 2.3 %copy-start = (f32[3]{0:T(128)S(1)}, f32[3]{0:T(128)}, u32[]{:S(2)}) copy-start(f32[3]{0:T(128)} %get-tuple-element.5) | copy-start | bytes 40

commit v3 on v2

--- a/solution.py
+++ b/solution.py
@@ -25,7 +25,7 @@
     nl, nr, count,
     psi_hbm, left_hbm, right_hbm, energies, coef_num, coef_den,
     out_hbm, ritz,
-    q, stage, left, right, right_t, acc, out_v, rows, cols,
+    q, stage, left, right, right_t, acc, out_v, local, rows, cols,
     send_sem, recv_sem, in_sem, rsend, rrecv, csend, crecv,
 ):
     na, nb, size, _ = psi_hbm.shape
@@ -133,7 +133,7 @@
     clear(has_hi_r, [(i, nb + 1) for i in range(1, na)])
     clear(has_lo_r, [(i, 0) for i in range(2, na + 1)])
 
-    rows[me_r] = jnp.zeros(rows.shape[1:], jnp.float32)
+    local[...] = jnp.zeros(local.shape, jnp.float32)
     partners = nr - 1 + nl - 1
     for other in (up_dn, dn_up, up_up, dn_dn):
         partners = partners + other.astype(jnp.int32)
@@ -152,18 +152,18 @@
             inner.astype(jnp.bfloat16), right_t[j, t], preferred_element_type=jnp.float32
         )
 
-    def gram(i, j):
-        total = jnp.zeros((size, size), jnp.float32)
-        for a in range(1, na + 1):
-            for b in range(1, nb + 1):
-                total += q[i, a, b].astype(jnp.float32) * q[j, a, b].astype(jnp.float32)
-        folded = jnp.sum(total, axis=0, keepdims=True)
-        part = folded[:, 0:128]
-        for lane in range(128, size, 128):
-            part = part + folded[:, lane : lane + 128]
-        rows[me_r, pl.ds(gram_row(i, j), 1), :] = part
-
-    gram(0, 0)
+    def gram(i, j, blocks):
+        part = jnp.zeros((1, size), jnp.float32)
+        for a, b in blocks:
+            part += jnp.sum(
+                q[i, a + 1, b + 1].astype(jnp.float32) * q[j, a + 1, b + 1].astype(jnp.float32),
+                axis=0, keepdims=True,
+            )
+        row = pl.ds(gram_row(i, j), 1)
+        for lane in range(0, size, 128):
+            local[row, :] += part[:, lane : lane + 128]
+
+    gram(0, 0, [(a, b) for a in range(na) for b in range(nb)])
 
     def is_local(t, i, j):
         if t < DIAG:
@@ -198,6 +198,9 @@
         def remote(i, j):
             return [t for t in range(DIAG, TERMS) if not is_local(t, i, j)]
 
+        def grams(blocks):
+            lax.fori_loop(0, k + 2, lambda i, c: (gram(i, k + 1, blocks), c)[1], 0)
+
         def onward(which):
             pl.when(k + 1 < ITERS)(lambda: send(k + 1, which))
 
@@ -207,6 +210,7 @@
             for j in range(nb):
                 finish(i, j, remote(i, j))
         onward((4, 5))
+        grams([(i, j) for i in range(1, na - 1) for j in range(nb)])
         receive(k, (0,))
         for j in range(nb - 1):
             finish(0, j, remote(0, j))
@@ -215,6 +219,7 @@
         for j in range(1, nb):
             finish(na - 1, j, remote(na - 1, j))
         onward((0, 7))
+        grams([(0, j) for j in range(nb - 1)] + [(na - 1, j) for j in range(1, nb)])
         receive(k, (1,))
         finish(0, nb - 1, remote(0, nb - 1))
         onward((9, 3))
@@ -222,7 +227,7 @@
         finish(na - 1, 0, remote(na - 1, 0))
         onward((8, 1))
 
-        lax.fori_loop(0, k + 2, lambda i, c: (gram(i, k + 1), c)[1], 0)
+        grams([(0, nb - 1), (na - 1, 0)])
         return carry
 
     lax.fori_loop(0, ITERS, step, 0)
@@ -246,13 +251,17 @@
             total = total + slots[n]
         return total
 
+    totals = jnp.sum(local[...], axis=1, keepdims=True)
+    place = lax.broadcasted_iota(jnp.int32, local.shape, 0)
+    lanes = lax.broadcasted_iota(jnp.int32, local.shape, 1)
+    rows[me_r] = jnp.sum(jnp.where(place == lanes, totals, 0.0), axis=0, keepdims=True)
     cols[me_l] = spread(rows, me_r, nr, lambda r: (me_l, r), rsend, rrecv)
     sums = spread(cols, me_l, nl, lambda l: (l, me_r), csend, crecv)
-    sums = jnp.sum(sums, axis=1, keepdims=True) * count
+    sums = sums * count
 
     def mean(i, j):
         row = gram_row(min(i, j), max(i, j))
-        return sums[row : row + 1, :]
+        return sums[:, row : row + 1]
 
     def product(x, y):
         total = jnp.zeros((1, 1), jnp.float32)
@@ -325,8 +334,9 @@
             pltpu.VMEM(right_env.shape, jnp.bfloat16),
             pltpu.VMEM(psi.shape, jnp.float32),
             pltpu.VMEM(psi.shape, jnp.bfloat16),
-            pltpu.VMEM((nr, GRAMS, 128), jnp.float32),
-            pltpu.VMEM((nl, GRAMS, 128), jnp.float32),
+            pltpu.VMEM((GRAMS, 128), jnp.float32),
+            pltpu.VMEM((nr, 1, 128), jnp.float32),
+            pltpu.VMEM((nl, 1, 128), jnp.float32),
             dma((ITERS, 10)),
             dma((ITERS, 10)),
             dma((max(3, na),)),

time: 49.8 us -> 49 us (0.984)
  Pallas kernels: 46.2 us -> 45.4 us
    pallas_call x1, Pallas kernels: 46.2 us -> 45.4 us  [per_device(): pl.pallas_call(functools.partial(kernel, nl, nr, count), out_shape=(jax.S...]
where the time goes in v3:
time: 49 us; the launch traced here: 48.8 us
  Pallas kernels  45.4 us (93%)
  local copies, waits for them, and re-layouts  2.78 us (6%)
  between operations  0.65 us (1%)
    pallas_call x1, Pallas kernels, per_device(): pl.pallas_call(functools.partial(kernel, nl, nr, count), out_shape=(jax.S...  45.4 us
    unnamed x4, local copies, waits for them, and re-layouts  2.78 us

profile of v3, /device:TPU:0, one launch (start us, length us, event | category | flops | bytes accessed | tf_op | source)
XLA Modules:
  0.0 48.8 jit_solution(4128151249848990977)
XLA Ops:
  0.6 45.4 %shard_map.77 = (bf16[4,2,256,256]{3,2,1,0:T(8,128)(2,1)}, f32[3]{0:T(128)}) custom-call(bf16[4,2,256,256]{3,2,1,0:T(8,128)(2,1)} %psi_hbm.1, bf16[4,4,256,256]{3,2,1,0:T(8,128)(2,1)} %left_hbm.1, bf16[2,4,256,256]{3,2,1,0:T(8,128)(2,1)} %right_hbm.1, f32[2,4]{1,0:T(2,128)} %bitcast.1, s32[2]{0:T(128)} %coef_num.1, s32[2]{0:T(128)} %coef_den.1), custom_call_target="tpu_custom_call" | custom-call | tf_op jit(solution)/shard_map/pallas_call | solution.py:321
  46.0 0.0 copy-start
  46.0 2.3 %copy.10 = bf16[4,2,256,256]{3,2,1,0:T(8,128)(2,1)} copy(bf16[4,2,256,256]{3,2,1,0:T(8,128)(2,1)} %get-tuple-element.4) | data formatting | bytes 2097152
  48.3 0.0 copy-done
  48.3 0.5 %copy.11 = f32[3]{0:T(128)} copy(f32[3]{0:T(128)S(1)} %copy-done) | data formatting | bytes 24
Async XLA Ops:
  46.0 2.3 %copy-start = (f32[3]{0:T(128)S(1)}, f32[3]{0:T(128)}, u32[]{:S(2)}) copy-start(f32[3]{0:T(128)} %get-tuple-element.5) | copy-start | bytes 40
